TPU v7x, 256 devices: a whole 4x4x8 slice. The times are simulated.
256 devices in a mesh: replica: 64 (over y, z, core), fsdp: 4 (over x).
Axes of the slice: x: 4, y: 4, z: 8, core: 2. Of those that a mesh axis runs over, the one named last changes fastest.
Arguments:
- activations: bfloat16 [64, 4096, 4096], P('replica', 'fsdp')
- cotangents: bfloat16 [64, 4096, 512], P('replica', 'fsdp'), may hold values from -0.059814453 to 0.059814453
- momentum: float32 [64, 4096, 512], P('replica', 'fsdp'), may hold values from -6 to 6
- keep_index: int32 [64, 512, 32], P(None, 'fsdp'), may hold values from 0 to 4095, as said below
Outputs:
- new_momentum: float32 [64, 4096, 512], P('replica', 'fsdp')
- update: bfloat16 [4096, 512], P('fsdp')
Inputs may be any that keep to these rules, and one draw needn't show every extreme that they name: keep_index[r, t, j] lies in [j * 64 * 2, (j + 1) * 64 * 2), so a tile's indices are distinct and ascending.
All inputs are finite; a program needn't handle non-finite values.
Results may differ from a plain program's by a relative error of at most 0.013.
Values may be sent and summed in bfloat16 or wider, within the bound.
A program may use at most 128 MiB of HBM per device.

v0:
```python
import jax
import jax.numpy as jnp
from jax import lax
from jax.sharding import Mesh
from jax.sharding import PartitionSpec as P

D_WIN = 4096
KV_WIN = 512
TILE = 64
KEEP = 32
REPLICA = ("replica_0", "replica_1", "replica_2")


BETA = 0.999
EPS = 1e-06
highest = lax.Precision.HIGHEST


def padded_to(lines, devices):
    spare = -lines.shape[0] % devices
    if not spare:
        return lines
    return jnp.concatenate([lines, jnp.zeros((spare, *lines.shape[1:]), lines.dtype)])


def from_everyone(x, axis):
    devices = lax.axis_size(axis)
    return lax.all_to_all(jnp.broadcast_to(x[None], (devices, *x.shape)), axis, 0, 0, tiled=True)


def laid_out(blocks, dim):
    blocks = jnp.moveaxis(blocks, 0, dim)
    shape = blocks.shape
    return blocks.reshape(*shape[:dim], shape[dim] * shape[dim + 1], *shape[dim + 2 :])


def gathered_by_axis(x, axes, dim):
    far, near = axes
    blocks = from_everyone(from_everyone(x, far), near)
    return laid_out(blocks.swapaxes(0, 1).reshape(-1, *x.shape), dim)


def in_blocks(x, dim, devices):
    shape = x.shape
    blocks = x.reshape(*shape[:dim], devices, shape[dim] // devices, *shape[dim + 1 :])
    return jnp.moveaxis(blocks, dim, 0)


def summed_on_arrival(x, axis, dim):
    blocks = in_blocks(x, dim, lax.axis_size(axis))
    arrived = lax.all_to_all(blocks, axis, split_axis=0, concat_axis=0, tiled=True)
    return arrived.sum(axis=0)


def summed_rows(x, axes, dim):
    far, near = axes
    blocks = in_blocks(x, dim, lax.axis_size(far))
    nearer = summed_on_arrival(blocks, near, dim + 1)
    arrived = lax.all_to_all(nearer, far, split_axis=0, concat_axis=0, tiled=True)
    return arrived.sum(axis=0)


def sum_by_parts(x, axes):
    lines = x.reshape(-1, x.shape[-1])
    padded = padded_to(lines, lax.axis_size(axes[0]) * lax.axis_size(axes[1]))
    whole = gathered_by_axis(summed_rows(padded, axes, 0), axes, 0)
    return lax.slice_in_dim(whole, 0, len(lines)).reshape(x.shape)


def of_everyone(x, axis):
    everything = from_everyone(x, axis)
    return jnp.sum(everything, axis=0)


def cosine_table():
    sample = jnp.arange(TILE).astype(jnp.float32)
    freq_index = sample[:, None]
    table = jnp.cos(jnp.pi * (2.0 * sample[None, :] + 1.0) * freq_index / (2.0 * TILE))
    weight_row = jnp.where(freq_index == 0, jnp.sqrt(1.0 / TILE), jnp.sqrt(2.0 / TILE))
    return table * weight_row


def forward_tiled(matrix, cosine):
    row_count, col_count = matrix.shape
    blocks = matrix.reshape(row_count // TILE, TILE, col_count // TILE, TILE)
    left = jnp.einsum("ka,iajb->ijkb", cosine, blocks, precision=highest)
    spectra = jnp.einsum("ijkb,lb->ijkl", left, cosine, precision=highest)
    band = TILE * TILE // KEEP
    return spectra.reshape(row_count // TILE * (col_count // TILE), KEEP, band)


def inverse_tiled(tiled, cosine, row_count, col_count):
    blocks = tiled.reshape(row_count // TILE, col_count // TILE, TILE, TILE)
    left = jnp.einsum("ka,ijkl->ijal", cosine, blocks, precision=highest)
    return jnp.einsum("ijal,lb->iajb", left, cosine, precision=highest).reshape(
        row_count, col_count
    )


def band_mask(indices):
    band = TILE * TILE // KEEP
    offsets = indices - jnp.arange(KEEP)[None, :] * band
    slots = jnp.arange(band)
    return (offsets[:, :, None] == slots[None, None, :]).astype(jnp.float32)


def shards(activations, cotangents, momentum, keep_index):
    cosine = cosine_table()
    tokens_here = activations[0]
    grads_here = cotangents[0]
    local_rows = momentum.shape[1]
    gradient = lax.psum_scatter(
        lax.dot_general(
            tokens_here, grads_here, (((0,), (0,)), ((), ())), preferred_element_type=jnp.float32
        ).astype(jnp.bfloat16),
        "fsdp",
        scatter_dimension=0,
        tiled=True,
    ).astype(jnp.float32)
    moment = BETA * momentum[0] + gradient
    spectrum = forward_tiled(moment, cosine)
    own_index = lax.dynamic_index_in_dim(keep_index, lax.axis_index(REPLICA), 0, keepdims=False)
    own_mask = band_mask(own_index)
    sent_tiles = spectrum * own_mask
    new_moment = moment - inverse_tiled(sent_tiles, cosine, local_rows, KV_WIN)
    summed = sum_by_parts(sent_tiles, (("replica_0", "replica_1"), "replica_2"))
    replica_count = lax.axis_size(REPLICA)
    merged = inverse_tiled(summed, cosine, local_rows, KV_WIN) / replica_count
    square_total = of_everyone(jnp.sum(merged * merged), "fsdp")
    scale_factor = lax.rsqrt(square_total / (D_WIN * KV_WIN) + EPS)
    update = (merged * scale_factor).astype(jnp.bfloat16)
    return (new_moment[None], update)


def solution(mesh):
    split = Mesh(
        mesh.devices.reshape(4, 8, 2, mesh.shape["fsdp"]),
        ("replica_0", "replica_1", "replica_2", "fsdp"),
    )
    in_specs = (
        P(REPLICA, "fsdp", None),
        P(REPLICA, "fsdp", None),
        P(REPLICA, "fsdp", None),
        P(None, "fsdp", None),
    )
    out_specs = (P(REPLICA, "fsdp", None), P("fsdp", None))
    return jax.shard_map(
        shards, mesh=split, in_specs=in_specs, out_specs=out_specs, check_vma=False
    )
```

profile of v0, /device:TPU:1, one launch (start us, length us, event | category | flops | bytes accessed | tf_op | source)
XLA Modules:
  0.0 235.1 jit_solution(5963626237717202013)
XLA Ops:
  7.2 0.0 copy-start
  7.2 0.0 reduce-scatter.2.cloned.1.call-start
  7.2 1.2 copy-done
  8.4 9.7 %fusion.2 = bf16[4096,512]{1,0:T(8,128)(2,1)} fusion(bf16[1,1024,4096]{2,1,0:T(8,128)(2,1)} %param.4, bf16[1,1024,512]{2,1,0:T(8,128)(2,1)S(1)} %copy-done), kind=kOutput, calls=%fused_computation.2 | convolution fusion | flops 4297064448 | bytes 13631488 | tf_op jit(solution)/shard_map/dot_general | solution.py:113
  18.1 0.0 reduce-scatter.2.cloned.1.call-update
  18.2 0.1 sub.26
  18.3 0.8 bitcast_subtract_fusion
  19.1 0.1 copy.56
  19.2 0.1 squeeze.16
  19.4 52.1 %reduce-scatter.2.cloned.1.call-done = bf16[1024,512]{1,0:T(8,128)(2,1)} async-done(((bf16[4096,512]{1,0:T(8,128)(2,1)}), bf16[1024,512]{1,0:T(8,128)(2,1)}) %reduce-scatter.2.cloned.1.call-update) | async-done | bytes 1048592 | tf_op jit(solution)/shard_map/reduce_scatter | solution.py:112
  71.4 2.2 bitcast_add_fusion
  73.7 2.4 %reshape.77 = f32[16,64,8,64]{3,2,1,0:T(8,128)} reshape(f32[1024,512]{1,0:T(8,128)S(1)} %bitcast_add_fusion) | data formatting | bytes 4194304 | tf_op jit(solution)/shard_map/reshape | solution.py:85
  76.0 9.2 %fusion.11 = f32[16,8,64,64]{3,2,1,0:T(8,128)S(1)} fusion(f32[16,64,8,64]{3,2,1,0:T(8,128)} %reshape.77, f32[64]{0:T(128)S(1)} %get-tuple-element.6, f32[64]{0:T(128)S(1)} %iota_convert_fusion, f32[64]{0:T(128)S(1)} %get-tuple-element.7), kind=kOutput, calls=%fused_computation.9 | convolution fusion | flops 402665472 | bytes 4195072 | tf_op jit(solution)/shard_map/ka,iajb->ijkb/dot_general | solution.py:86
  85.3 8.4 %fusion.9 = f32[16,8,64,64]{3,2,1,0:T(8,128)} fusion(f32[16,8,64,64]{3,2,1,0:T(8,128)S(1)} %fusion.11, f32[64]{0:T(128)S(1)} %get-tuple-element.6, f32[64]{0:T(128)S(1)} %iota_convert_fusion, f32[64]{0:T(128)S(1)} %get-tuple-element.7), kind=kOutput, calls=%fused_computation.7 | convolution fusion | flops 402665472 | bytes 4195072 | tf_op jit(solution)/shard_map/ijkb,lb->ijkl/dot_general | solution.py:87
  93.7 4.6 %reshape.79 = f32[32,2,64,128]{3,2,1,0:T(8,128)} reshape(f32[16,8,64,64]{3,2,1,0:T(8,128)} %fusion.9) | data formatting | bytes 4194304 | tf_op jit(solution)/shard_map/reshape | solution.py:89
  98.3 1.9 fusion.20
  100.2 6.7 %all_to_all.26 = f32[2,32,64,128]{3,2,1,0:T(8,128)} all-to-all(f32[2,32,64,128]{3,2,1,0:T(8,128)S(1)} %fusion.20), channel_id=1, replica_groups=mesh['replica_0'=4,'replica_1'=8,'replica_2'=2,'fsdp'=4] {'replica_2'}, dimensions={0} | all-to-all | bytes 4194304 | tf_op jit(solution)/shard_map/all_to_all | solution.py:51
  106.9 1.8 reduce_sum.36
  108.8 34.7 %all_to_all.27 = f32[32,64,128]{2,1,0:T(8,128)} all-to-all(f32[32,64,128]{2,1,0:T(8,128)S(1)} %reduce_sum.36), channel_id=1, replica_groups=mesh['replica_0'=4,'replica_1'=8,'replica_2'=2,'fsdp'=4] {'replica_0','r..., dimensions={0} | all-to-all | bytes 2097152 | tf_op jit(solution)/shard_map/all_to_all | solution.py:59
  143.5 1.3 reduce_sum.37
  144.8 1.1 broadcast_in_dim.19
  145.8 8.0 %all-to-all-start.2 = ((f32[32,64,128]{2,1,0:T(8,128)}), f32[32,64,128]{2,1,0:T(8,128)S(1)}, u32[]{:S(2)}, u32[]{:S(2)}) async-start(f32[32,64,128]{2,1,0:T(8,128)} %broadcast_in_dim.19), calls=%async_computation.3 | async-start | bytes 2097152 | tf_op jit(solution)/shard_map/all_to_all | solution.py:28
  153.9 1.1 eq.59
  155.0 1.3 copy.47
  156.3 10.1 %fusion.13 = f32[16,8,64,64]{3,2,1,0:T(8,128)S(1)} fusion(f32[16,8,64,64]{3,2,1,0:T(8,128)} %fusion.9, s32[64,64]{1,0:T(8,128)S(1)} %bitcast.70, s32[16,8,64]{2,1,0:T(8,128)S(1)} %copy.47, f32[64]{0:T(128)S(1)} %get-tuple-element.6, f32[64]{0:T(128)S(1)} %iota_convert_fusion, f32[64]{0:T(128)S(1)} %get-tuple-element.7), kind=kOutput, calls=%fused_computation.13 | convolution fusion | flops 403714048 | bytes 4244224 | tf_op jit(solution)/shard_map/ka,ijkl->ijal/dot_general | solution.py:94
  166.4 5.5 %fusion.16 = f32[16,64,8,64]{1,3,2,0:T(8,128)} fusion(f32[16,8,64,64]{3,2,1,0:T(8,128)S(1)} %fusion.13, f32[64]{0:T(128)S(1)} %get-tuple-element.6, f32[64]{0:T(128)S(1)} %iota_convert_fusion, f32[64]{0:T(128)S(1)} %get-tuple-element.7), kind=kOutput, calls=%fused_computation.16 | convolution fusion | flops 402665472 | bytes 4195072 | tf_op jit(solution)/shard_map/ijal,lb->iajb/dot_general | solution.py:95
  172.0 5.3 %copy.55 = f32[16,64,8,64]{3,2,1,0:T(8,128)} copy(f32[16,64,8,64]{1,3,2,0:T(8,128)} %fusion.16) | data formatting | bytes 4194304 | tf_op jit(solution)/shard_map/ijal,lb->iajb/transpose | solution.py:95
  177.3 4.8 %reshape.78 = f32[1024,512]{1,0:T(8,128)} reshape(f32[16,64,8,64]{3,2,1,0:T(8,128)} %copy.55) | data formatting | bytes 4194304 | tf_op jit(solution)/shard_map/reshape | solution.py:95
  182.1 3.4 %subtract_bitcast_fusion = f32[1,1024,512]{2,1,0:T(8,128)} fusion(f32[1024,512]{1,0:T(8,128)S(1)} %bitcast_add_fusion, f32[1024,512]{1,0:T(8,128)} %reshape.78), kind=kLoop, calls=%fused_computation.22 | loop fusion | flops 524288 | bytes 6291456 | tf_op jit(solution)/shard_map/broadcast_in_dim | solution.py:132
  185.5 0.0 all-to-all-done.2
  185.5 0.2 broadcast_in_dim.20
  185.7 6.6 %all_to_all.28 = f32[2,32,64,128]{3,2,1,0:T(8,128)S(1)} all-to-all(f32[2,32,64,128]{3,2,1,0:T(8,128)S(1)} %broadcast_in_dim.20), channel_id=1, replica_groups=mesh['replica_0'=4,'replica_1'=8,'replica_2'=2,'fsdp'=4] {'replica_2'}, dimensions={0} | all-to-all | bytes 4194304 | tf_op jit(solution)/shard_map/all_to_all | solution.py:28
  192.3 0.1 copy.59
  192.4 2.3 reshape_reshape_reshape_reshape.3
  194.7 8.7 %fusion.25 = f32[16,8,64,64]{3,2,1,0:T(8,128)S(1)} fusion(f32[16,8,64,64]{3,2,1,0:T(8,128)} %reshape_reshape_reshape_reshape.3, f32[64]{0:T(128)S(1)} %get-tuple-element.6, f32[64]{0:T(128)S(1)} %iota_convert_fusion, f32[64]{0:T(128)S(1)} %get-tuple-element.7), kind=kOutput, calls=%fused_computation.27 | convolution fusion | flops 402665472 | bytes 4195072 | tf_op jit(solution)/shard_map/ka,ijkl->ijal/dot_general | solution.py:94
  203.4 6.6 %multiply_reduce_fusion = (f32[]{:T(128)}, f32[64,16,8,64]{3,0,2,1:T(8,128)}) fusion(f32[16,8,64,64]{3,2,1,0:T(8,128)S(1)} %fusion.25, f32[64]{0:T(128)S(1)} %get-tuple-element.6, f32[64]{0:T(128)S(1)} %iota_convert_fusion, f32[64]{0:T(128)S(1)} %get-tuple-element.7), kind=kOutput, calls=%fused_computation.12 | convolution fusion | flops 404238336 | bytes 4195076 | tf_op jit(solution)/shard_map/ijal,lb->iajb/dot_general | solution.py:95
  210.1 0.6 broadcast_in_dim.21
  210.7 6.5 %all_to_all.29 = f32[4,1,1]{2,1,0:T(1,128)S(1)} all-to-all(f32[4,1,1]{2,1,0:T(1,128)S(1)} %broadcast_in_dim.21), channel_id=1, replica_groups=mesh['replica_0'=4,'replica_1'=8,'replica_2'=2,'fsdp'=4] {'fsdp'}, dimensions={0} | all-to-all | bytes 32 | tf_op jit(solution)/shard_map/all_to_all | solution.py:28
  217.2 0.6 reduce_sum.39
  218.5 0.0 copy-start.1
  218.5 2.8 %fusion.19 = bf16[16,64,8,64]{1,3,2,0:T(8,128)(2,1)S(1)} fusion(f32[64,16,8,64]{3,0,2,1:T(8,128)} %get-tuple-element.5, f32[]{:T(128)S(6)} %mul.180), kind=kLoop, calls=%fused_computation.17 | loop fusion | flops 1048576 | bytes 3145732 | tf_op jit(solution)/shard_map/convert_element_type | solution.py:131
  221.4 2.8 %copy.64 = bf16[16,64,8,64]{3,2,1,0:T(8,128)(2,1)} copy(bf16[16,64,8,64]{1,3,2,0:T(8,128)(2,1)S(1)} %fusion.19) | data formatting | bytes 2097152 | tf_op jit(solution)/shard_map/convert_element_type | solution.py:131
  224.2 4.0 %convert_element_type.45 = bf16[1024,512]{1,0:T(8,128)(2,1)} reshape(bf16[16,64,8,64]{3,2,1,0:T(8,128)(2,1)} %copy.64) | data formatting | bytes 2097152 | tf_op jit(solution)/shard_map/convert_element_type | solution.py:131
  228.2 0.0 copy-done.1
  (9 shorter events, 0.1 us)
Async XLA Ops:
  7.2 1.2 copy-start
  7.2 64.2 %reduce-scatter.2.cloned.1.call-start = ((), (), s32[]{:S(2)}) async-start(), calls=%async_computation.6 | async-start | bytes 5242880 | tf_op jit(solution)/shard_map/reduce_scatter | solution.py:112
  145.8 39.6 %all-to-all-start.2 = ((f32[32,64,128]{2,1,0:T(8,128)}), f32[32,64,128]{2,1,0:T(8,128)S(1)}, u32[]{:S(2)}, u32[]{:S(2)}) async-start(f32[32,64,128]{2,1,0:T(8,128)} %broadcast_in_dim.19), calls=%async_computation.3 | async-start | bytes 2097152 | tf_op jit(solution)/shard_map/all_to_all | solution.py:28
  218.5 9.8 %copy-start.1 = (bf16[1,1024,512]{2,1,0:T(8,128)(2,1)S(1)}, bf16[1,1024,512]{2,1,0:T(8,128)(2,1)}, u32[]{:S(2)}) copy-start(bf16[1,1024,512]{2,1,0:T(8,128)(2,1)} %param.5) | copy-start | bytes 3145732
Sparse Core Ops, SparseCore 0:
  18.3 53.0 reduce-scatter.1
where the time goes:
time: 236 us; the launch traced here: 235 us
  matrix products  58.3 us (25%)
  blocking collectives  54.4 us (23%)
  waiting for transfers between devices  52.1 us (22%)
  local copies, waits for them, and re-layouts  32.2 us (14%)
  other arithmetic  15 us (6%)
  between operations  14.9 us (6%)
  starting transfers between devices  8.08 us (3%)
    reduce_scatter x1, waiting for transfers between devices, shards(): lax.psum_scatter(lax.dot_general(tokens_here, grads_here, (((0,), (0,)),...  52.1 us
    all_to_all x1, blocking collectives, summed_rows(): lax.all_to_all(nearer, far, split_axis=0, concat_axis=0, tiled=True)  34.7 us
    dot_general x2, matrix products, inverse_tiled(): left = jnp.einsum('ka,ijkl->ijal', cosine, blocks, precision=highest)  18.8 us
    all_to_all x2, blocking collectives, from_everyone(): lax.all_to_all(jnp.broadcast_to(x[None], (devices, *x.shape)), axis, 0, 0...  13 us
    dot_general x2, matrix products, inverse_tiled(): jnp.einsum('ijal,lb->iajb', left, cosine, precision=highest)  12.2 us
    dot_general x1, matrix products, shards(): lax.dot_general(tokens_here, grads_here, (((0,), (0,)), ((), ())), prefer...  9.75 us
    dot_general x1, matrix products, forward_tiled(): left = jnp.einsum('ka,iajb->ijkb', cosine, blocks, precision=highest)  9.22 us
    dot_general x1, matrix products, forward_tiled(): spectra = jnp.einsum('ijkb,lb->ijkl', left, cosine, precision=highest)  8.4 us
  transfers between devices with their start and end apart: 2, of which 1 were waited for; matrix products, arithmetic and copies ran while one was open for 14% of the time, Pallas kernels for 0%

commit v1 on v0

v1 whole, which is shorter than its diff:
```python
import functools

import jax
import jax.numpy as jnp
import numpy as np
from jax import lax
from jax.experimental import pallas as pl
from jax.experimental.pallas import tpu as pltpu
from jax.sharding import Mesh
from jax.sharding import PartitionSpec as P

D_WIN = 4096
KV_WIN = 512
TILE = 64
KEEP = 32
REPLICA = ("y", "z", "c")
BETA = 0.999
EPS = 1e-06
NX, NY, NZ, NC = 4, 4, 8, 2
NR = NY * NZ * NC
TOK = 1024
ROWS = D_WIN // NX
HALF = ROWS // 2
CH = 128
C = HALF // CH
SKEW = 2
MESH = pl.DeviceIdType.MESH
F32, BF16 = jnp.float32, jnp.bfloat16
NN = (((1,), (0,)), ((), ()))
NT = (((1,), (1,)), ((), ()))
TN = (((0,), (0,)), ((), ()))


def tables():
    n = np.arange(TILE, dtype=np.float64)
    cosine = np.cos(np.pi * (2.0 * n[None, :] + 1.0) * n[:, None] / (2.0 * TILE))
    cosine *= np.where(n[:, None] == 0, np.sqrt(1.0 / TILE), np.sqrt(2.0 / TILE))
    cosine = cosine.astype(np.float32)
    forward = np.kron(np.eye(4, dtype=np.float32), cosine)
    merge = [
        np.kron(np.eye(4, dtype=np.float32), cosine[b::2]) / np.float32(NR)
        for b in range(2)
    ]
    parts = [forward, forward.T, np.concatenate(merge)]
    out = []
    for part in parts:
        head = part.astype(jnp.bfloat16)
        out += [head, (part - head.astype(np.float32)).astype(jnp.bfloat16)]
    return np.concatenate(out)


def mm(a, b, dims=NN):
    return lax.dot_general(a, b, dims, preferred_element_type=F32)


def split(x):
    head = x.astype(BF16)
    return head, (x - head.astype(F32)).astype(BF16)


def left3(head, rest, x):
    xh, xl = split(x)
    return mm(head, xh) + mm(head, xl) + mm(rest, xh)


def right3(x, head, rest):
    xh, xl = split(x)
    return mm(xh, head) + mm(xl, head) + mm(xh, rest)


def iota(shape, dim):
    return lax.broadcasted_iota(jnp.int32, shape, dim)


def kernel(
    act, cot, mom, keep, cst, out_m, out_u,
    actv, cotv, momv, keepv, kown, cstv, bmat, psum_v, offs,
    send, recv, newm, vz, vy, upd, ufin, sqacc, sqbuf,
    act_sem, in_sem, mom_sem, rs_send, rs_recv, z_send, z_recv, y_send, y_recv,
    sw_send, sw_recv, n_send, n_recv, om_sem, ou_sem,
):
    y, z, c, x = (lax.axis_index(a) for a in ("y", "z", "c", "x"))
    me = (y * NZ + z) * NC + c

    def block_of(h, d):
        return lax.rem(jnp.where(d == 0, x + 3 * (1 + h), x + 1 + h), NX)

    def act_copy(h, d, k):
        col = block_of(h, d) * ROWS + d * HALF + k * CH
        return pltpu.make_async_copy(
            act.at[0, :, pl.ds(pl.multiple_of(col, CH), CH)],
            actv.at[h, d, k],
            act_sem.at[h, d, k],
        )

    def mom_copy(d, k):
        row = pl.multiple_of(d * HALF + k * CH, CH)
        return pltpu.make_async_copy(
            mom.at[0, pl.ds(row, CH)], momv.at[d, k], mom_sem.at[d, k]
        )

    small = [
        pltpu.make_async_copy(cot.at[0], cotv, in_sem.at[0]),
        pltpu.make_async_copy(cst, cstv, in_sem.at[1]),
        pltpu.make_async_copy(keep.at[me], kown, in_sem.at[2]),
        pltpu.make_async_copy(
            keep.at[:, pl.ds(pl.multiple_of(c * 64, 64), 64)], keepv, in_sem.at[3]
        ),
    ]
    small[0].start()

    def start_act(i, _):
        h, k, d = i // (2 * C), lax.rem(i // 2, C), lax.rem(i, 2)
        act_copy(h, d, k).start()
        return _

    lax.fori_loop(0, 2 * C, start_act, 0)

    barrier = pltpu.get_barrier_semaphore()
    peers = []
    for i in range(1, NX * NC):
        o = lax.rem(x * NC + c + i, NX * NC)
        peers.append({"x": o // NC, "c": lax.rem(o, NC)})
    z_peers = [{"z": lax.rem(z + i, NZ)} for i in range(1, NZ)]
    y_peers = []
    for i in range(1, NY * NC):
        o = lax.rem(y * NC + c + i, NY * NC)
        y_peers.append((o // NC, lax.rem(o, NC)))
    for dev in peers + z_peers + [{"y": a, "c": b} for a, b in y_peers]:
        pl.semaphore_signal(barrier, inc=1, device_id=dev, device_id_type=MESH)

    for copy in small[1:3]:
        copy.start()
    lax.fori_loop(2 * C, 8 * C, start_act, 0)

    def start_mom(i, _):
        mom_copy(lax.rem(i, 2), i // 2).start()
        return _

    lax.fori_loop(0, 2 * C, start_mom, 0)
    small[3].start()

    bmat[...] = (iota((16, 512), 0) % 8 == iota((16, 512), 1) // TILE).astype(F32).astype(BF16)
    ki, li = iota((128, 256), 0), iota((128, 256), 1)
    psum_v[...] = (
        ((ki // 64) == (li // 128)) & ((ki % 64) // 2 == li % 32)
    ).astype(F32).astype(BF16)
    sqacc[...] = jnp.zeros_like(sqacc)

    def rs_copy(h, d, k):
        to = lax.rem(jnp.where(d == 0, x + 1, x + 3), NX)
        return pltpu.make_async_remote_copy(
            src_ref=send.at[h, d, k],
            dst_ref=recv.at[h, d, k],
            send_sem=rs_send.at[h, d, k],
            recv_sem=rs_recv.at[h, d, k],
            device_id={"x": to},
            device_id_type=MESH,
        )

    def own_part(h, d, k):
        act_copy(h, d, k).wait()
        return mm(actv[h, d, k], cotv[...], TN)

    def first(k):
        def one(d, _):
            send[0, d, k] = own_part(0, d, k).astype(BF16)
            rs_copy(0, d, k).start()
            return _

        lax.fori_loop(0, 2, one, 0)

    def hop(h, k):
        def one(d, _):
            part = own_part(h, d, k)
            rs_copy(h - 1, d, k).wait_recv()
            send[h, d, k] = (part + recv[h - 1, d, k].astype(F32)).astype(BF16)
            rs_copy(h, d, k).start()
            return _

        lax.fori_loop(0, 2, one, 0)

    def z_copy(k, i):
        return pltpu.make_async_remote_copy(
            src_ref=vz.at[k, :, z],
            dst_ref=vz.at[k, :, z],
            send_sem=z_send.at[k, i - 1],
            recv_sem=z_recv.at[k, i - 1],
            device_id={"z": lax.rem(z + i, NZ)},
            device_id_type=MESH,
        )

    def y_copy(k, i):
        a, b = y_peers[i - 1]
        return pltpu.make_async_remote_copy(
            src_ref=vz.at[k, b],
            dst_ref=vy.at[k, y * NC + c],
            send_sem=y_send.at[k, i - 1],
            recv_sem=y_recv.at[k, i - 1],
            device_id={"y": a, "c": b},
            device_id_type=MESH,
        )

    def swap_copy(k):
        row = pl.ds(pl.multiple_of(c * HALF + k * CH, CH), CH)
        return pltpu.make_async_remote_copy(
            src_ref=upd.at[row],
            dst_ref=upd.at[row],
            send_sem=sw_send.at[k],
            recv_sem=sw_recv.at[k],
            device_id={"c": 1 - c},
            device_id_type=MESH,
        )

    def norm_copy(i):
        return pltpu.make_async_remote_copy(
            src_ref=sqbuf.at[x * NC + c],
            dst_ref=sqbuf.at[x * NC + c],
            send_sem=n_send.at[i - 1],
            recv_sem=n_recv.at[i - 1],
            device_id=peers[i - 1],
            device_id_type=MESH,
        )

    def out_copy(d, k):
        row = pl.multiple_of(d * HALF + k * CH, CH)
        return pltpu.make_async_copy(
            newm.at[d, k], out_m.at[0, pl.ds(row, CH)], om_sem.at[d, k]
        )

    fh, fl = cstv.at[0:256], cstv.at[256:512]
    th, tl = cstv.at[512:768], cstv.at[768:1024]
    qh, ql = cstv.at[1024:1280], cstv.at[1280:1536]

    def finish(k):
        def one(d, _):
            part = own_part(3, d, k)
            mom_copy(d, k).wait()
            rs_copy(2, d, k).wait_recv()
            moment = BETA * momv[d, k] + (part + recv[2, d, k].astype(F32))
            half = left3(fh[0:128, 0:128], fl[0:128, 0:128], moment)
            spec = jnp.concatenate(
                [right3(half[:, i : i + 256], th[...], tl[...]) for i in (0, 256)], axis=1
            )
            base = pl.multiple_of(d * 64 + k * 16, 16)
            own = (kown[pl.ds(base, 16), :] - iota((16, KEEP), 1) * 128).astype(F32)
            pick = (iota((128, KEEP), 0) % 64 // 2 == iota((128, KEEP), 1)).astype(F32)
            rows = mm(pick.astype(BF16), own.astype(BF16), NT)
            same = iota((128, 16), 0) // 64 == iota((128, 16), 1) // 8
            slot = mm(jnp.where(same, rows, 0.0).astype(BF16), bmat[...])
            here = (iota((128, 512), 0) % 2 * 64 + iota((128, 512), 1) % 64).astype(F32)
            sent = jnp.where(slot == here, spec, 0.0)
            back = left3(th[0:128, 0:128], tl[0:128, 0:128], sent)
            newm[d, k] = moment - jnp.concatenate(
                [right3(back[:, i : i + 256], fh[...], fl[...]) for i in (0, 256)], axis=1
            )
            out_copy(d, k).start()
            sh, sl = split(sent)
            bm = bmat[0:8, :]
            by_row = mm(bm, sh, NT) + mm(bm, sl, NT)
            bh, bl = split(by_row)
            by_band = mm(bh, psum_v[...]) + mm(bl, psum_v[...])
            ti, lane = iota((8, 256), 0), iota((8, 256), 1)
            by_band = jnp.where(lane % 128 // 32 == ti // 2, by_band, 0.0)
            for q in range(2):
                line = jnp.sum(
                    jnp.where(ti % 2 == q, by_band, 0.0), axis=0, keepdims=True
                )
                for t in range(2):
                    vz[k, d, z, pl.ds(2 * t + q, 1), :] = line[:, t * 128 : t * 128 + 128]
            return _

        lax.fori_loop(0, 2, one, 0)
        for i in range(1, NZ):
            z_copy(k, i).start()

    def spread(k):
        for i in range(1, NZ):
            z_copy(k, i).wait_recv()
        for i in range(1, NY * NC):
            y_copy(k, i).start()
        vy[k, y * NC + c] = vz[k, c]

    def gather_offsets():
        small[3].wait()
        band = iota((8, 128), 1) % 32 * 128

        def one(r, _):
            for q in range(2):
                parts = [keepv[r, pl.ds(2 * m + q, 8, stride=8), :] for m in range(4)]
                offs[r, pl.ds(8 * q, 8), :] = jnp.concatenate(parts, axis=1) - band
            return _

        lax.fori_loop(0, NR, one, 0)

    def merge(k):
        for i in range(1, NY * NC):
            y_copy(k, i).wait_recv()
        place = iota((128, 128), 0)
        for t in range(2):
            sides = []
            for q in range(2):
                line = 8 * q + 2 * k + t

                def add(g, total, line=line, t=t, q=q):
                    a, b = g // NC, lax.rem(g, NC)
                    for zz in range(NZ):
                        r = (a * NZ + zz) * NC + b
                        o = offs[r, pl.ds(line, 1), :]
                        v = vy[k, g, zz, pl.ds(2 * t + q, 1), :]
                        total += jnp.where(o == place, v, 0.0)
                    return total

                total = lax.fori_loop(0, NY * NC, add, jnp.zeros((128, 128), F32))
                left = left3(th[0:128, 0:128], tl[0:128, 0:128], total)
                sides.append(
                    right3(left[0:64], qh[0:128], ql[0:128])
                    + right3(left[64:128], qh[128:256], ql[128:256])
                )
            tiles = jnp.concatenate(sides, axis=0).T
            row = pl.ds(pl.multiple_of(c * HALF + k * CH + t * 64, 64), 64)
            for m in range(4):
                piece = tiles[m * 64 : m * 64 + 64]
                upd[row, m * 128 : m * 128 + 128] = piece.astype(BF16)
                sqacc[...] += jnp.sum((piece * piece).reshape(8, 8, 128), axis=0)
        swap_copy(k).start()

    def step(t, carry):
        for h, unit in ((0, first), (1, hop), (2, hop), (3, finish)):
            k = t - SKEW * h

            @pl.when((k >= 0) & (k < C))
            def _(h=h, k=k, unit=unit):
                unit(h, k) if unit is hop else unit(k)

        @pl.when(t == 2)
        def _():
            gather_offsets()

        k1 = t - SKEW * 3 - 1

        @pl.when((k1 >= 0) & (k1 < C))
        def _():
            spread(k1)

        k2 = t - SKEW * 3 - 2

        @pl.when((k2 >= 0) & (k2 < C))
        def _():
            merge(k2)

        return carry

    small[0].wait()
    small[1].wait()
    small[2].wait()
    n_peers = len(peers) + len(z_peers) + len(y_peers)
    pl.semaphore_wait(barrier, n_peers)
    lax.fori_loop(0, C + SKEW * 3 + 2, step, 0)

    sqbuf[x * NC + c] = sqacc[...]
    for i in range(1, NX * NC):
        norm_copy(i).start()
    for k in range(C):
        swap_copy(k).wait_recv()
    for i in range(1, NX * NC):
        norm_copy(i).wait_recv()
    total = jnp.sum(jnp.sum(sqbuf[...], axis=0), keepdims=True)
    scale = lax.rsqrt(total / (D_WIN * KV_WIN) + EPS)

    def u_copy(i):
        row = pl.ds(pl.multiple_of(i * 128, 128), 128)
        return pltpu.make_async_copy(ufin.at[row], out_u.at[row], ou_sem.at[i])

    def scaled(i, _):
        row = pl.ds(pl.multiple_of(i * 128, 128), 128)
        ufin[row] = (upd[row].astype(F32) * scale).astype(BF16)
        u_copy(i).start()
        return _

    lax.fori_loop(0, ROWS // 128, scaled, 0)

    def drain(k, _):
        for d in range(2):
            out_copy(d, k).wait()
            for h in range(3):
                rs_copy(h, d, k).wait_send()
        for i in range(1, NZ):
            z_copy(k, i).wait_send()
        for i in range(1, NY * NC):
            y_copy(k, i).wait_send()
        swap_copy(k).wait_send()
        return _

    lax.fori_loop(0, C, drain, 0)
    for i in range(1, NX * NC):
        norm_copy(i).wait_send()
    lax.fori_loop(0, ROWS // 128, lambda i, _: (u_copy(i).wait(), _)[1], 0)


def shards(activations, cotangents, momentum, keep_index):
    constants = jnp.asarray(tables())
    dma = pltpu.SemaphoreType.DMA
    vmem = pltpu.VMEM
    return pl.pallas_call(
        kernel,
        out_shape=(
            jax.ShapeDtypeStruct((1, ROWS, KV_WIN), F32),
            jax.ShapeDtypeStruct((ROWS, KV_WIN), BF16),
        ),
        in_specs=[pl.BlockSpec(memory_space=pl.ANY)] * 5,
        out_specs=[pl.BlockSpec(memory_space=pl.ANY)] * 2,
        scratch_shapes=[
            vmem((4, 2, C, TOK, CH), BF16),
            vmem((TOK, KV_WIN), BF16),
            vmem((2, C, CH, KV_WIN), F32),
            vmem((NR, 64, KEEP), jnp.int32),
            vmem((128, KEEP), jnp.int32),
            vmem((1536, 256), BF16),
            vmem((16, 512), BF16),
            vmem((128, 256), BF16),
            vmem((NR, 16, 128), jnp.int32),
            vmem((3, 2, C, CH, KV_WIN), BF16),
            vmem((3, 2, C, CH, KV_WIN), BF16),
            vmem((2, C, CH, KV_WIN), F32),
            vmem((C, 2, NZ, 4, 128), F32),
            vmem((C, NY * NC, NZ, 4, 128), F32),
            vmem((ROWS, KV_WIN), BF16),
            vmem((ROWS, KV_WIN), BF16),
            vmem((8, 128), F32),
            vmem((NX * NC, 8, 128), F32),
            dma((4, 2, C)),
            dma((4,)),
            dma((2, C)),
            dma((3, 2, C)),
            dma((3, 2, C)),
            dma((C, NZ - 1)),
            dma((C, NZ - 1)),
            dma((C, NY * NC - 1)),
            dma((C, NY * NC - 1)),
            dma((C,)),
            dma((C,)),
            dma((NX * NC - 1,)),
            dma((NX * NC - 1,)),
            dma((2, C)),
            dma((ROWS // 128,)),
        ],
        compiler_params=pltpu.CompilerParams(
            collective_id=0, has_side_effects=True, vmem_limit_bytes=56 * 2**20
        ),
    )(activations, cotangents, momentum, keep_index, constants)


def solution(mesh):
    split_mesh = Mesh(
        mesh.devices.reshape(NY, NZ, NC, NX),
        ("y", "z", "c", "x"),
    )
    in_specs = (
        P(REPLICA, "x", None),
        P(REPLICA, "x", None),
        P(REPLICA, "x", None),
        P(None, "x", None),
    )
    out_specs = (P(REPLICA, "x", None), P("x", None))
    return jax.shard_map(
        shards, mesh=split_mesh, in_specs=in_specs, out_specs=out_specs, check_vma=False
    )
```

time: 236 us -> 85.7 us (0.36)
  Pallas kernels: 0 us -> 77.2 us
  matrix products: 58.3 us -> 0 us
  blocking collectives: 54.4 us -> 0 us
  waiting for transfers between devices: 52.1 us -> 0 us
  local copies, waits for them, and re-layouts: 32.2 us -> 7.73 us
  other arithmetic: 15 us -> 0 us
  between operations: 14.9 us -> 0.65 us
  starting transfers between devices: 8.08 us -> 0 us
    pallas_call x0 -> x1, Pallas kernels: none -> 77.2 us  [shards(): pl.pallas_call(kernel, out_shape=(jax.ShapeDtypeStruct((1, ROWS, KV_WIN),...]
    dot_general x7 -> x0, matrix products: 58.3 us -> none  [the longest x2 18.8 us: inverse_tiled(): left = jnp.einsum('ka,ijkl->ijal', cosine, blocks, precision=highest)]
    all_to_all x4 -> x0, blocking collectives: 54.4 us -> none  [the longest x1 34.7 us: summed_rows(): lax.all_to_all(nearer, far, split_axis=0, concat_axis=0, tiled=True)]
    reduce_scatter x1 -> x0, waiting for transfers between devices: 52.1 us -> none  [shards(): lax.psum_scatter(lax.dot_general(tokens_here, grads_here, (((0,), (0,)),...]
    reshape x3 -> x0, local copies, waits for them, and re-layouts: 11.7 us -> none  [the longest x1 4.77 us: inverse_tiled(): jnp.einsum('ijal,lb->iajb', left, cosine, precision=highest)]
    all_to_all x1 -> x0, starting transfers between devices: 8.04 us -> none  [from_everyone(): lax.all_to_all(jnp.broadcast_to(x[None], (devices, *x.shape)), axis, 0, 0...]
    convert_element_type x2 -> x0, local copies, waits for them, and re-layouts: 6.88 us -> none  [shards(): update = (merged * scale_factor).astype(jnp.bfloat16)]
    unnamed x4 -> x5, local copies, waits for them, and re-layouts: 1.19 us -> 7.73 us
  transfers between devices with their start and end apart: 2 -> 0, of which waited for: 1 -> 0; matrix products, arithmetic and copies ran while one was open for 14% -> 0% of each run, Pallas kernels for 0% -> 0%
where the time goes in v1:
time: 85.7 us; the launch traced here: 85.6 us
  Pallas kernels  77.2 us (90%)
  local copies, waits for them, and re-layouts  7.73 us (9%)
    pallas_call x1, Pallas kernels, shards(): pl.pallas_call(kernel, out_shape=(jax.ShapeDtypeStruct((1, ROWS, KV_WIN),...  77.2 us
    unnamed x5, local copies, waits for them, and re-layouts  7.73 us

profile of v1, /device:TPU:1, one launch (start us, length us, event | category | flops | bytes accessed | tf_op | source)
XLA Modules:
  0.0 85.6 jit_solution(12834415877603197348)
XLA Ops:
  0.6 3.6 %copy.7.keep = s32[64,128,32]{2,1,0:T(8,128)} copy(s32[64,128,32]{1,2,0:T(8,128)} %param.8) | data formatting | bytes 2097152 | tf_op args[3]
  4.2 77.2 %shard_map.68 = (f32[1,1024,512]{2,1,0:T(8,128)}, bf16[1024,512]{1,0:T(8,128)(2,1)}) custom-call(bf16[1,1024,4096]{2,1,0:T(8,128)(2,1)} %act.1, bf16[1,1024,512]{2,1,0:T(8,128)(2,1)} %cot.1, f32[1,1024,512]{2,1,0:T(8,128)} %mom.1, s32[64,128,32]{2,1,0:T(8,128)} %copy.7.keep, bf16[1536,256]{1,0:T(8,128)(2,1)} %constant.2.clone.cst), custom_call_target="tpu_custom_call" | custom-call | tf_op jit(solution)/shard_map/pallas_call | solution.py:405
  81.4 0.0 copy-start
  81.4 3.2 %copy.10 = f32[1,1024,512]{2,1,0:T(8,128)} copy(f32[1,1024,512]{2,1,0:T(8,128)} %get-tuple-element.4) | data formatting | bytes 4194304
  84.6 0.0 copy-done
  84.6 1.0 %copy.11 = bf16[1024,512]{1,0:T(8,128)(2,1)} copy(bf16[1024,512]{1,0:T(8,128)(2,1)S(1)} %copy-done) | data formatting | bytes 2097152
Async XLA Ops:
  81.4 3.2 %copy-start = (bf16[1024,512]{1,0:T(8,128)(2,1)S(1)}, bf16[1024,512]{1,0:T(8,128)(2,1)}, u32[]{:S(2)}) copy-start(bf16[1024,512]{1,0:T(8,128)(2,1)} %get-tuple-element.5) | copy-start | bytes 3145732

commit v2 on v1

v2 whole, which is shorter than its diff:
```python
import functools

import jax
import jax.numpy as jnp
import numpy as np
from jax import lax
from jax.experimental import pallas as pl
from jax.experimental.pallas import tpu as pltpu
from jax.sharding import Mesh
from jax.sharding import PartitionSpec as P

D_WIN = 4096
KV_WIN = 512
TILE = 64
KEEP = 32
REPLICA = ("y", "z", "c")
BETA = 0.999
EPS = 1e-06
NX, NY, NZ, NC = 4, 4, 8, 2
NR = NY * NZ * NC
TOK = 1024
ROWS = D_WIN // NX
HALF = ROWS // 2
CH = 128
C = HALF // CH
FIRST = (0, 1, 4, 5)
HOP1 = (2, 3, 7, 8)
HOP2 = (4, 5, 9, 10)
FINISH = (6, 7, 10, 11)
SPREAD = (7, 9, 11, 12)
MERGE = (9, 11, 12, 13)
MESH = pl.DeviceIdType.MESH
F32, BF16 = jnp.float32, jnp.bfloat16
NN = (((1,), (0,)), ((), ()))
NT = (((1,), (1,)), ((), ()))
TN = (((0,), (0,)), ((), ()))


def tables():
    n = np.arange(TILE, dtype=np.float64)
    cosine = np.cos(np.pi * (2.0 * n[None, :] + 1.0) * n[:, None] / (2.0 * TILE))
    cosine *= np.where(n[:, None] == 0, np.sqrt(1.0 / TILE), np.sqrt(2.0 / TILE))
    cosine = cosine.astype(np.float32)
    forward = np.kron(np.eye(4, dtype=np.float32), cosine)
    merge = [
        np.kron(np.eye(4, dtype=np.float32), cosine[b::2]) / np.float32(NR)
        for b in range(2)
    ]
    parts = [forward, forward.T, np.concatenate(merge)]
    out = []
    for part in parts:
        head = part.astype(jnp.bfloat16)
        out += [head, (part - head.astype(np.float32)).astype(jnp.bfloat16)]
    return np.concatenate(out)


def mm(a, b, dims=NN):
    return lax.dot_general(a, b, dims, preferred_element_type=F32)


def split(x):
    head = x.astype(BF16)
    return head, (x - head.astype(F32)).astype(BF16)


def left3(both, x):
    xh, xl = split(x)
    n = both.shape[0] // 2
    wide = mm(both, xh)
    return wide[:n] + wide[n:] + mm(both[:n], xl)


def right3(x, head, rest):
    xh, xl = split(x)
    n = x.shape[0]
    tall = mm(jnp.concatenate([xh, xl], axis=0), head)
    return tall[:n] + tall[n:] + mm(xh, rest)


def iota(shape, dim):
    return lax.broadcasted_iota(jnp.int32, shape, dim)


def kernel(
    act, cot, mom, keep, cst, out_m, upd, out_s,
    actv, cotv, momv, keepv, cstv, pick_v, bmat, over_v, psum_v, offs,
    send, recv, vz, vy, sqacc, sqbuf,
    act_sem, in_sem, mom_sem, rs_send, rs_recv, z_send, z_recv, y_send, y_recv,
    sw_send, sw_recv, n_send, n_recv,
):
    y, z, c, x = (lax.axis_index(a) for a in ("y", "z", "c", "x"))
    me = (y * NZ + z) * NC + c

    def block_of(h, d):
        return lax.rem(jnp.where(d == 0, x + 3 * (1 + h), x + 1 + h), NX)

    def act_copy(h, d, k):
        col = block_of(h, d) * ROWS + d * HALF + k * CH
        return pltpu.make_async_copy(
            act.at[0, :, pl.ds(pl.multiple_of(col, CH), CH)],
            actv.at[h, k, :, pl.ds(pl.multiple_of(d * CH, CH), CH)],
            act_sem.at[h, d, k],
        )

    def mom_copy(d, k):
        row = pl.multiple_of(d * HALF + k * CH, CH)
        return pltpu.make_async_copy(
            mom.at[0, pl.ds(row, CH)], momv.at[d, k], mom_sem.at[d, k]
        )

    small = [
        pltpu.make_async_copy(cst, cstv, in_sem.at[0]),
        pltpu.make_async_copy(keep, keepv, in_sem.at[1]),
        pltpu.make_async_copy(cot.at[0], cotv, in_sem.at[2]),
    ]

    barrier = pltpu.get_barrier_semaphore()
    peers = []
    for i in range(1, NX * NC):
        o = lax.rem(x * NC + c + i, NX * NC)
        peers.append({"x": o // NC, "c": lax.rem(o, NC)})
    z_peers = [{"z": lax.rem(z + i, NZ)} for i in range(1, NZ)]
    y_peers = []
    for i in range(1, NY * NC):
        o = lax.rem(y * NC + c + i, NY * NC)
        y_peers.append((o // NC, lax.rem(o, NC)))
    for dev in peers + z_peers + [{"y": a, "c": b} for a, b in y_peers]:
        pl.semaphore_signal(barrier, inc=1, device_id=dev, device_id_type=MESH)

    def start_act(i, carry):
        h, k, d = i // (2 * C), lax.rem(i // 2, C), lax.rem(i, 2)
        act_copy(h, d, k).start()
        return carry

    small[2].start()
    lax.fori_loop(0, 2 * C, start_act, 0)
    small[0].start()
    small[1].start()
    lax.fori_loop(2 * C, 8 * C, start_act, 0)

    def start_mom(i, carry):
        mom_copy(lax.rem(i, 2), i // 2).start()
        return carry

    lax.fori_loop(0, 2 * C, start_mom, 0)

    def prepare():
        one = lambda mask: mask.astype(F32).astype(BF16)
        bmat[...] = one(iota((8, 256), 0) == iota((8, 256), 1) // TILE)
        over_v[...] = one(iota((128, 256), 0) % 4 == iota((128, 256), 1) // TILE)
        ki, li = iota((512, 512), 0), iota((512, 512), 1)
        psum_v[...] = one(
            (ki % 256 // 64 == li // 128)
            & (ki % 64 // 2 == li % 32)
            & (ki // 256 == li % 128 // 64)
        )
        row, tile = iota((64, 128), 0), iota((64, 128), 1)
        part, row = row // 16, row % 16
        want = c * 64 + row // 4 * 16 + row // 2 % 2 * 8 + part * 2 + row % 2
        pick_v[...] = one(want == tile)
        sqacc[...] = jnp.zeros_like(sqacc)

    def rs_copy(h, d, k):
        to = lax.rem(jnp.where(d == 0, x + 1, x + 3), NX)
        return pltpu.make_async_remote_copy(
            src_ref=send.at[h, d, k],
            dst_ref=recv.at[h, d, k],
            send_sem=rs_send.at[h, d, k],
            recv_sem=rs_recv.at[h, d, k],
            device_id={"x": to},
            device_id_type=MESH,
        )

    def own_part(h, k):
        for d in range(2):
            act_copy(h, d, k).wait()
        return mm(actv[h, k], cotv[...], TN)

    def first(k):
        part = own_part(0, k).astype(BF16)
        for d in range(2):
            send[0, d, k] = part[d * CH : d * CH + CH]
            rs_copy(0, d, k).start()

    def hop(h, k):
        part = own_part(h, k)
        for d in range(2):
            rs_copy(h - 1, d, k).wait_recv()
            mine = part[d * CH : d * CH + CH]
            send[h, d, k] = (mine + recv[h - 1, d, k].astype(F32)).astype(BF16)
            rs_copy(h, d, k).start()

    def z_copy(k, i):
        return pltpu.make_async_remote_copy(
            src_ref=vz.at[k, :, z],
            dst_ref=vz.at[k, :, z],
            send_sem=z_send.at[k, i - 1],
            recv_sem=z_recv.at[k, i - 1],
            device_id={"z": lax.rem(z + i, NZ)},
            device_id_type=MESH,
        )

    def y_copy(k, i):
        a, b = y_peers[i - 1]
        return pltpu.make_async_remote_copy(
            src_ref=vz.at[k, b],
            dst_ref=vy.at[k, y * NC + c],
            send_sem=y_send.at[k, i - 1],
            recv_sem=y_recv.at[k, i - 1],
            device_id={"y": a, "c": b},
            device_id_type=MESH,
        )

    def swap_copy(k):
        row = pl.ds(pl.multiple_of(c * HALF + k * CH, CH), CH)
        return pltpu.make_async_remote_copy(
            src_ref=upd.at[row],
            dst_ref=upd.at[row],
            send_sem=sw_send.at[k],
            recv_sem=sw_recv.at[k],
            device_id={"c": 1 - c},
            device_id_type=MESH,
        )

    def norm_copy(i):
        return pltpu.make_async_remote_copy(
            src_ref=sqbuf.at[x * NC + c],
            dst_ref=sqbuf.at[x * NC + c],
            send_sem=n_send.at[i - 1],
            recv_sem=n_recv.at[i - 1],
            device_id=peers[i - 1],
            device_id_type=MESH,
        )

    fh, fl = cstv.at[0:256], cstv.at[256:512]
    th, tl = cstv.at[512:768], cstv.at[768:1024]
    qh, ql = cstv.at[1024:1280], cstv.at[1280:1536]

    def finish(k):
        @pl.when(k == 0)
        def _():
            small[0].wait()
            small[1].wait()

        part = own_part(3, k)
        for d in range(2):
            mom_copy(d, k).wait()
        own = (keepv[me] - iota((KEEP, 128), 0) * 128).astype(F32).astype(BF16)
        pick = (iota((64, KEEP), 0) // 2 == iota((64, KEEP), 1)).astype(F32).astype(BF16)
        slot = jnp.concatenate([mm(pick, own)] * 8, axis=0)
        ki, tile = iota((512, 128), 0), iota((512, 128), 1)
        slab, d, tr = ki // 256, ki // 128 % 2, ki // 64 % 2
        mine = (tile // 8 == d * 8 + k * 2 + tr) & (tile % 8 // 4 == slab)
        slot = mm(jnp.where(mine, slot, 0.0).astype(BF16), over_v[...])
        here = (iota((512, 256), 0) % 2 * 64 + iota((512, 256), 1) % TILE).astype(F32)
        old = jnp.concatenate([momv[0, k], momv[1, k]], axis=0)
        for d in range(2):
            rs_copy(2, d, k).wait_recv()
        got = jnp.concatenate([recv[2, 0, k], recv[2, 1, k]], axis=0).astype(F32)
        moment = BETA * old + (part + got)
        half = left3(cstv[0:512], moment)
        half = jnp.concatenate([half[:, 0:256], half[:, 256:512]], axis=0)
        sent = jnp.where(slot == here, right3(half, th[...], tl[...]), 0.0)
        by_row = mm(bmat[...], sent.astype(BF16), NT).astype(BF16)
        by_band = mm(by_row, psum_v[...])
        ti, lane = iota((8, 512), 0), iota((8, 512), 1)
        by_band = jnp.where(lane % 64 // 32 == ti // 2, by_band, 0.0)
        for q in range(2):
            line = jnp.sum(jnp.where(ti % 2 == q, by_band, 0.0), axis=0, keepdims=True)
            for d in range(2):
                for t in range(2):
                    at = d * 256 + t * 128
                    vz[k, d, z, 2 * t + q : 2 * t + q + 1, :] = line[:, at : at + 128]
        for i in range(1, NZ):
            z_copy(k, i).start()
        back = right3(sent, fh[...], fl[...])
        back = jnp.concatenate([back[0:256], back[256:512]], axis=1)
        new = moment - left3(cstv[512:1024], back)
        for d in range(2):
            row = pl.ds(pl.multiple_of(d * HALF + k * CH, CH), CH)
            out_m[0, row] = new[d * CH : d * CH + CH]

    def spread(k):
        for i in range(1, NZ):
            z_copy(k, i).wait_recv()
        for i in range(1, NY * NC):
            y_copy(k, i).start()
        vy[k, y * NC + c] = vz[k, c]

    def gather_offsets():
        def one(i, carry):
            four = keepv[pl.ds(4 * i, 4)] - iota((4, KEEP, 128), 1) * 128
            four = four.reshape(4 * KEEP, 128).astype(F32).astype(BF16)
            got = mm(pick_v[...], four, NT)
            for r in range(4):
                parts = [
                    got[16 * p : 16 * p + 16, 32 * r : 32 * r + 32] for p in range(4)
                ]
                offs[4 * i + r] = jnp.concatenate(parts, axis=1)
            return carry

        lax.fori_loop(0, NR // 4, one, 0, unroll=8)

    def merge(k):
        for i in range(1, NY * NC):
            y_copy(k, i).wait_recv()
        place = iota((128, 128), 0).astype(F32).astype(BF16)
        none = jnp.zeros((128, 128), BF16)
        totals = []
        for t in range(2):

            def add(g, pair, t=t):
                a, b = g // NC, lax.rem(g, NC)
                pair = list(pair)
                for zz in range(0, NZ, 4):
                    for q in range(2):
                        hits = []
                        for z4 in range(zz, zz + 4):
                            r = (a * NZ + z4) * NC + b
                            o = offs[r, pl.ds(4 * k + 2 * t + q, 1), :]
                            v = vy[k, g, z4, 2 * t + q : 2 * t + q + 1, :]
                            o, v = (
                                jnp.broadcast_to(w, (16, 128)).astype(BF16) for w in (o, v)
                            )
                            o, v = (jnp.concatenate([w] * 8, axis=0) for w in (o, v))
                            hits.append(jnp.where(o == place, v, none))
                        four = (hits[0] + hits[1]) + (hits[2] + hits[3])
                        pair[q] += four.astype(F32)
                return tuple(pair)

            zero = jnp.zeros((128, 128), F32)
            totals += lax.fori_loop(0, NY * NC, add, (zero, zero))
        square = sum(jnp.sum((a * a).reshape(16, 8, 128), axis=0) for a in totals)
        sqacc[...] += square

        @pl.when(k == C - 1)
        def _():
            sqbuf[x * NC + c] = sqacc[...]
            for i in range(1, NX * NC):
                norm_copy(i).start()

        table = jnp.concatenate([th[0:128, 0:128], tl[0:128, 0:128]], axis=0)
        left = left3(table, jnp.concatenate(totals, axis=1))
        left = jnp.concatenate(
            [
                jnp.concatenate([left[0:64, i : i + 128], left[64:128, i : i + 128]], axis=1)
                for i in range(0, 512, 128)
            ],
            axis=0,
        )
        both = right3(left, qh[...], ql[...])
        for t in range(2):
            tiles = both[t * 128 : t * 128 + 128].T
            row = pl.ds(pl.multiple_of(c * HALF + k * CH + t * 64, 64), 64)
            for m in range(4):
                piece = tiles[m * 64 : m * 64 + 64]
                upd[row, m * 128 : m * 128 + 128] = piece.astype(BF16)
        swap_copy(k).start()

    def step(t, carry):
        def at(times, unit):
            hit = [t == when for when in times]
            k = sum(jnp.where(h, i, 0) for i, h in enumerate(hit))

            @pl.when(functools.reduce(jnp.logical_or, hit))
            def _():
                unit(k)

        at(HOP2, functools.partial(hop, 2))
        at(HOP1, functools.partial(hop, 1))
        at(FIRST, first)
        at(FINISH, finish)

        @pl.when(t == 1)
        def _():
            prepare()

        @pl.when(t == 6)
        def _():
            gather_offsets()

        at(SPREAD, spread)
        at(MERGE, merge)
        return carry

    small[2].wait()
    pl.semaphore_wait(barrier, len(peers) + len(z_peers) + len(y_peers))
    lax.fori_loop(0, MERGE[-1] + 1, step, 0)

    def drain(k, carry):
        for d in range(2):
            for h in range(3):
                rs_copy(h, d, k).wait_send()
        for i in range(1, NZ):
            z_copy(k, i).wait_send()
        for i in range(1, NY * NC):
            y_copy(k, i).wait_send()
        swap_copy(k).wait_send()
        return carry

    lax.fori_loop(0, C, drain, 0)
    for k in range(C):
        swap_copy(k).wait_recv()
    for i in range(1, NX * NC):
        norm_copy(i).wait_recv()
    for i in range(1, NX * NC):
        norm_copy(i).wait_send()
    total = jnp.sum(jnp.sum(sqbuf[...], axis=0), keepdims=True)
    out_s[...] = jnp.broadcast_to(
        lax.rsqrt(total / (NR * NR) / (D_WIN * KV_WIN) + EPS), (8, 128)
    )


def write_out(new_v, upd_v, scale_v, out_m, out_u, done, m_sem, u_sem):
    half = ROWS // 2
    m_copies = [
        pltpu.make_async_copy(
            new_v.at[0, i * half : i * half + half],
            out_m.at[0, i * half : i * half + half],
            m_sem.at[i],
        )
        for i in range(2)
    ]
    for copy in m_copies:
        copy.start()
    scale = scale_v[0:1, 0:1]
    part = ROWS // 4
    u_copies = []
    for i in range(4):
        row = slice(i * part, i * part + part)
        done[row] = (upd_v[row].astype(F32) * scale).astype(BF16)
        u_copies.append(pltpu.make_async_copy(done.at[row], out_u.at[row], u_sem.at[i]))
        u_copies[-1].start()
    for copy in m_copies + u_copies:
        copy.wait()


def shards(activations, cotangents, momentum, keep_index):
    operands = (
        activations,
        cotangents,
        momentum,
        keep_index.swapaxes(1, 2),
        jnp.asarray(tables()),
    )
    dma = pltpu.SemaphoreType.DMA
    vmem = pltpu.VMEM
    new, update, scale = pl.pallas_call(
        kernel,
        out_shape=(
            jax.ShapeDtypeStruct((1, ROWS, KV_WIN), F32),
            jax.ShapeDtypeStruct((ROWS, KV_WIN), BF16),
            jax.ShapeDtypeStruct((8, 128), F32),
        ),
        in_specs=[pl.BlockSpec(memory_space=pl.ANY)] * 5,
        out_specs=[pl.BlockSpec(memory_space=pltpu.VMEM)] * 3,
        scratch_shapes=[
            vmem((4, C, TOK, 2 * CH), BF16),
            vmem((TOK, KV_WIN), BF16),
            vmem((2, C, CH, KV_WIN), F32),
            vmem((NR, KEEP, 128), jnp.int32),
            vmem((1536, 256), BF16),
            vmem((64, 128), BF16),
            vmem((8, 256), BF16),
            vmem((128, 256), BF16),
            vmem((512, 512), BF16),
            vmem((NR, 16, 128), F32),
            vmem((3, 2, C, CH, KV_WIN), BF16),
            vmem((3, 2, C, CH, KV_WIN), BF16),
            vmem((C, 2, NZ, 4, 128), F32),
            vmem((C, NY * NC, NZ, 4, 128), F32),
            vmem((8, 128), F32),
            vmem((NX * NC, 8, 128), F32),
            dma((4, 2, C)),
            dma((3,)),
            dma((2, C)),
            dma((3, 2, C)),
            dma((3, 2, C)),
            dma((C, NZ - 1)),
            dma((C, NZ - 1)),
            dma((C, NY * NC - 1)),
            dma((C, NY * NC - 1)),
            dma((C,)),
            dma((C,)),
            dma((NX * NC - 1,)),
            dma((NX * NC - 1,)),
        ],
        compiler_params=pltpu.CompilerParams(
            collective_id=0, has_side_effects=True, vmem_limit_bytes=48 * 2**20
        ),
    )(*(pltpu.with_memory_space_constraint(a, pltpu.HBM) for a in operands))
    return pl.pallas_call(
        write_out,
        out_shape=(
            jax.ShapeDtypeStruct((1, ROWS, KV_WIN), F32),
            jax.ShapeDtypeStruct((ROWS, KV_WIN), BF16),
        ),
        in_specs=[pl.BlockSpec(memory_space=pltpu.VMEM)] * 3,
        out_specs=[pl.BlockSpec(memory_space=pl.ANY)] * 2,
        scratch_shapes=[vmem((ROWS, KV_WIN), BF16), dma((2,)), dma((4,))],
        compiler_params=pltpu.CompilerParams(vmem_limit_bytes=16 * 2**20),
    )(new, update, scale)


def solution(mesh):
    split_mesh = Mesh(
        mesh.devices.reshape(NY, NZ, NC, NX),
        ("y", "z", "c", "x"),
    )
    in_specs = (
        P(REPLICA, "x", None),
        P(REPLICA, "x", None),
        P(REPLICA, "x", None),
        P(None, "x", None),
    )
    out_specs = (P(REPLICA, "x", None), P("x", None))
    return jax.shard_map(
        shards, mesh=split_mesh, in_specs=in_specs, out_specs=out_specs, check_vma=False
    )
```

time: 85.7 us -> 68.1 us (0.79)
  Pallas kernels: 77.2 us -> 67.4 us
  local copies, waits for them, and re-layouts: 7.73 us -> 0 us
    pallas_call x1, Pallas kernels: 77.2 us -> 65.7 us  [shards(): pl.pallas_call(kernel, out_shape=(jax.ShapeDtypeStruct((1, ROWS, KV_WIN),...]
    unnamed x5 -> x0, local copies, waits for them, and re-layouts: 7.73 us -> none
    pallas_call x0 -> x1, Pallas kernels: none -> 1.71 us  [shards(): pl.pallas_call(write_out, out_shape=(jax.ShapeDtypeStruct((1, ROWS, KV_WI...]
where the time goes in v2:
time: 68.1 us; the launch traced here: 68 us
  Pallas kernels  67.4 us (99%)
    pallas_call x1, Pallas kernels, shards(): pl.pallas_call(kernel, out_shape=(jax.ShapeDtypeStruct((1, ROWS, KV_WIN),...  65.7 us
    pallas_call x1, Pallas kernels, shards(): pl.pallas_call(write_out, out_shape=(jax.ShapeDtypeStruct((1, ROWS, KV_WI...  1.71 us

profile of v2, /device:TPU:1, one launch (start us, length us, event | category | flops | bytes accessed | tf_op | source)
XLA Modules:
  0.0 68.0 jit_solution(4948855040201239546)
XLA Ops:
  0.6 65.7 %shard_map.68 = (f32[1,1024,512]{2,1,0:T(8,128)S(1)}, bf16[1024,512]{1,0:T(8,128)(2,1)S(1)}, f32[8,128]{1,0:T(8,128)S(1)}) custom-call(bf16[1,1024,4096]{2,1,0:T(8,128)(2,1)} %act.1, bf16[1,1024,512]{2,1,0:T(8,128)(2,1)} %cot.1, f32[1,1024,512]{2,1,0:T(8,128)} %mom.1, s32[64,32,128]{2,1,0:T(8,128)} %bitcast.1, bf16[1536,256]{1,0:T(8,128)(2,1)} %constant.2.clone.cst), custom_call_target="tpu_custom_call" | custom-call | tf_op jit(solution)/shard_map/pallas_call | solution.py:448
  66.3 1.7 %shard_map.69 = (f32[1,1024,512]{2,1,0:T(8,128)}, bf16[1024,512]{1,0:T(8,128)(2,1)}) custom-call(f32[1,1024,512]{2,1,0:T(8,128)S(1)} %get-tuple-element.5.new_v, bf16[1024,512]{1,0:T(8,128)(2,1)S(1)} %get-tuple-element.6.upd_v, f32[8,128]{1,0:T(8,128)S(1)} %get-tuple-element.7.scale_v), custom_call_target="tpu_custom_call" | custom-call | tf_op jit(solution)/shard_map/pallas_call | solution.py:492

commit v3 on v2

--- a/solution.py
+++ b/solution.py
@@ -176,11 +176,18 @@
             act_copy(h, d, k).wait()
         return mm(actv[h, k], cotv[...], TN)
 
+    def first_part(k):
+        part = own_part(0, k).astype(BF16)
+        for d in range(2):
+            send[0, d, k] = part[d * CH : d * CH + CH]
+
+    def first_send(k):
+        for d in range(2):
+            rs_copy(0, d, k).start()
+
     def first(k):
-        part = own_part(0, k).astype(BF16)
-        for d in range(2):
-            send[0, d, k] = part[d * CH : d * CH + CH]
-            rs_copy(0, d, k).start()
+        first_part(k)
+        first_send(k)
 
     def hop(h, k):
         part = own_part(h, k)
@@ -371,10 +378,6 @@
         at(FIRST, first)
         at(FINISH, finish)
 
-        @pl.when(t == 1)
-        def _():
-            prepare()
-
         @pl.when(t == 6)
         def _():
             gather_offsets()
@@ -384,8 +387,13 @@
         return carry
 
     small[2].wait()
+    first_part(0)
+    first_part(1)
     pl.semaphore_wait(barrier, len(peers) + len(z_peers) + len(y_peers))
-    lax.fori_loop(0, MERGE[-1] + 1, step, 0)
+    first_send(0)
+    first_send(1)
+    prepare()
+    lax.fori_loop(2, MERGE[-1] + 1, step, 0)
 
     def drain(k, carry):
         for d in range(2):

time: 68.1 us -> 67.8 us (level)
  no operation moved by 1% of the time
where the time goes in v3:
time: 67.8 us; the launch traced here: 67.7 us
  Pallas kernels  67.1 us (99%)
    pallas_call x1, Pallas kernels, shards(): pl.pallas_call(kernel, out_shape=(jax.ShapeDtypeStruct((1, ROWS, KV_WIN),...  65.4 us
    pallas_call x1, Pallas kernels, shards(): pl.pallas_call(write_out, out_shape=(jax.ShapeDtypeStruct((1, ROWS, KV_WI...  1.71 us

profile of v3, /device:TPU:1, one launch (start us, length us, event | category | flops | bytes accessed | tf_op | source)
XLA Modules:
  0.0 67.7 jit_solution(17245729919457718031)
XLA Ops:
  0.6 65.4 %shard_map.68 = (f32[1,1024,512]{2,1,0:T(8,128)S(1)}, bf16[1024,512]{1,0:T(8,128)(2,1)S(1)}, f32[8,128]{1,0:T(8,128)S(1)}) custom-call(bf16[1,1024,4096]{2,1,0:T(8,128)(2,1)} %act.1, bf16[1,1024,512]{2,1,0:T(8,128)(2,1)} %cot.1, f32[1,1024,512]{2,1,0:T(8,128)} %mom.1, s32[64,32,128]{2,1,0:T(8,128)} %bitcast.1, bf16[1536,256]{1,0:T(8,128)(2,1)} %constant.2.clone.cst), custom_call_target="tpu_custom_call" | custom-call | tf_op jit(solution)/shard_map/pallas_call | solution.py:456
  66.0 1.7 %shard_map.69 = (f32[1,1024,512]{2,1,0:T(8,128)}, bf16[1024,512]{1,0:T(8,128)(2,1)}) custom-call(f32[1,1024,512]{2,1,0:T(8,128)S(1)} %get-tuple-element.5.new_v, bf16[1024,512]{1,0:T(8,128)(2,1)S(1)} %get-tuple-element.6.upd_v, f32[8,128]{1,0:T(8,128)S(1)} %get-tuple-element.7.scale_v), custom_call_target="tpu_custom_call" | custom-call | tf_op jit(solution)/shard_map/pallas_call | solution.py:500
